TPU v7x, 32 devices: a whole 2x2x4 slice. The times are simulated.
32 devices in a mesh: tm: 4 (over x, core), chan: 8 (over z, y).
Axes of the slice: x: 2, y: 2, z: 4, core: 2. Of those that a mesh axis runs over, the one named last changes fastest.
Arguments:
- raw_blocks: bfloat16 [16, 5120, 1024], P('tm', 'chan'), may hold values from -6 to 6
- fir_taps: bfloat16 [128], replicated, may hold values from -0.5 to 0.5
- recorder_channel: int32 [5120], replicated, may hold values from 0 to 5119, as said below
- pairs: int32 [4096, 2], P('chan'), may hold values from 0 to 5119, as said below
Outputs:
- stacks: float32 [4096, 256], P('chan')
Inputs may be any that keep to these rules, and one draw needn't show every extreme that they name: `recorder_channel`: A permutation of the channels; each aligned block of 640 recorder rows holds exactly 80 channels of every range of 640 consecutive channels. `pairs`: each aligned block of 512 rows names exactly 32 distinct channels of every range of 640 consecutive channels.
All inputs are finite; a program needn't handle non-finite values.
Results may differ from a plain program's by a relative error of at most 0.0084.
Values may be sent and summed in bfloat16 or wider, within the bound.
No kernel may reach another device: no remote copies, remote signals or barrier semaphores. Data moves between devices by JAX's collectives and lax.ppermute only.
A program may use at most 128 MiB of HBM per device.

v0:
```python
import jax
import jax.numpy as jnp
from jax import lax
from jax.sharding import PartitionSpec as P

NB = 128
SMOOTH = 4


def make_fir(fir_taps, length):
    taps_n = fir_taps.shape[0]
    period = taps_n + length
    padded = jnp.concatenate([fir_taps.astype(jnp.float32), jnp.zeros((length,), jnp.float32)])
    repeated = jnp.tile(padded, length)[: length * (period - 1)].reshape(length, period - 1)[
        :, :length
    ]
    return repeated.astype(jnp.bfloat16)


def make_table(length, bin_count):
    samples = jnp.arange(length, dtype=jnp.int32)
    freqs = jnp.arange(1, bin_count + 1, dtype=jnp.int32)
    phase_idx = samples[:, None] * freqs[None, :] % length
    angles = phase_idx.astype(jnp.float32) * (2.0 * jnp.pi / length)
    return jnp.concatenate([jnp.cos(angles), -jnp.sin(angles)], axis=1).astype(jnp.bfloat16)


def make_smooth(bin_count, half_width):
    places = jnp.arange(bin_count, dtype=jnp.int32)
    band_mask = (jnp.abs(places[:, None] - places[None, :]) <= half_width).astype(jnp.float32)
    return band_mask / jnp.sum(band_mask, axis=0, keepdims=True)


def whiten(spectrum, smoother):
    bin_count = spectrum.shape[-1] // 2
    real_part = spectrum[..., :bin_count]
    imag_part = spectrum[..., bin_count:]
    magnitude = jnp.sqrt(real_part * real_part + imag_part * imag_part)
    smoothed = jnp.dot(magnitude, smoother, precision=lax.Precision.HIGHEST)
    mean_level = jnp.mean(magnitude, axis=-1, keepdims=True)
    divisor = smoothed + 0.1 * mean_level + 1e-06
    return (spectrum / jnp.concatenate([divisor, divisor], axis=-1)).astype(jnp.bfloat16)


def cross(left_rows, right_rows):
    bin_count = left_rows.shape[-1] // 2
    left_f = left_rows.astype(jnp.float32)
    right_f = right_rows.astype(jnp.float32)
    left_re, left_im = (left_f[..., :bin_count], left_f[..., bin_count:])
    right_re, right_im = (right_f[..., :bin_count], right_f[..., bin_count:])
    real_out = left_re * right_re + left_im * right_im
    imag_out = left_im * right_re - left_re * right_im
    return jnp.concatenate([real_out, imag_out], axis=-1)


def local(raw_blocks, fir_taps, recorder_channel, pairs):
    windows, ch_dev, length = raw_blocks.shape
    rows_of = jnp.argsort(recorder_channel, stable=True)
    endpoints = jnp.concatenate([pairs[:, 0], pairs[:, 1]])
    wanted_ids = jnp.take(rows_of, endpoints)
    fir_matrix = make_fir(fir_taps, length)
    dft_table = make_table(length, NB)
    smoother = make_smooth(NB, SMOOTH)
    flat_rows = raw_blocks.reshape(windows * ch_dev, length)
    filtered = jnp.dot(flat_rows, fir_matrix, preferred_element_type=jnp.float32).astype(
        jnp.bfloat16
    )
    spectrum = jnp.dot(filtered, dft_table, preferred_element_type=jnp.float32)
    whitened = whiten(spectrum, smoother).reshape(windows, ch_dev, 2 * NB)
    pair_count = pairs.shape[0]
    empty = jnp.zeros((windows, 2 * pair_count, 2 * NB), jnp.bfloat16)
    part_rows = lax.all_gather(whitened, "chan", axis=1, tiled=True)
    inside = (wanted_ids >= 0) & (wanted_ids < part_rows.shape[1])
    taken = jnp.take(part_rows, jnp.clip(wanted_ids, 0, part_rows.shape[1] - 1), axis=1)
    chosen = jnp.where(inside[None, :, None], taken, empty)
    products = cross(chosen[:, :pair_count], chosen[:, pair_count:])
    stacked = jnp.sum(products, axis=0)
    summed = lax.psum(stacked, "tm")
    return summed / (windows * lax.axis_size("tm"))


def solution(mesh):
    in_specs = (P("tm", "chan", None), P(), P(), P("chan", None))
    out_specs = P("chan", None)
    return jax.shard_map(local, mesh=mesh, in_specs=in_specs, out_specs=out_specs, check_vma=False)
```

profile of v0, /device:TPU:0, one launch (start us, length us, event | category | flops | bytes accessed | tf_op | source)
XLA Modules:
  0.0 248.1 jit_solution(11060469899976761753)
XLA Ops:
  6.5 0.0 all-gather.2.cloned.1.call-start
  6.6 2.2 cosine_convert_fusion
  8.8 0.7 concatenate.69
  9.5 0.2 tile.10
  9.7 3.8 %tile.11 = bf16[1179648]{0:T(1024)(128)(2,1)} reshape(bf16[1024,1152]{1,0:T(8,128)(2,1)S(1)} %tile.10) | data formatting | bytes 4718592 | tf_op jit(solution)/shard_map/tile | solution.py:14
  13.5 0.0 slice-start
  13.5 1.7 slice-done
  15.2 6.4 %reshape.232 = bf16[1024,1151]{1,0:T(8,128)(2,1)} reshape(bf16[1178624]{0:T(1024)(128)(2,1)S(1)} %slice-done) | data formatting | bytes 4714496 | tf_op jit(solution)/shard_map/reshape | solution.py:14
  21.5 10.3 %fusion.6 = f32[2560,256]{1,0:T(8,128)S(1)} fusion(bf16[2560,1024]{1,0:T(8,128)(2,1)} %bitcast.16, bf16[1024,1151]{1,0:T(8,128)(2,1)} %reshape.232, bf16[1024,128]{1,0:T(8,128)(2,1)S(1)} %get-tuple-element.16, bf16[1024,128]{1,0:T(8,128)(2,1)S(1)} %get-tuple-element.15), kind=kOutput, calls=%fused_computation.14 | convolution fusion | flops 6714556416 | bytes 10485760 | tf_op jit(solution)/shard_map/dot_general | solution.py:68
  31.9 0.5 fusion.17
  32.4 1.5 fusion
  33.9 0.5 fusion.1
  34.4 0.0 copy-start
  34.5 0.0 copy-start.1
  34.5 2.1 copy.11
  36.6 0.0 all-gather.2.cloned.1.call-update
  36.6 0.0 all-reduce.3.cloned.1.call-start
  36.6 0.0 copy-done
  36.6 6.8 %sort.17 = (s32[5120]{0:T(1024)}, s32[5120]{0:T(1024)S(1)}) sort(s32[5120]{0:T(1024)S(1)} %copy-done, s32[5120]{0:T(1024)S(1)} %iota.22), dimensions={0}, to_apply=%region_0.0 | sort | flops 66560 | bytes 81920 | tf_op jit(solution)/shard_map/jit(argsort)/sort | solution.py:58
  43.4 0.0 copy-done.1
  43.4 6.4 %gather_fusion = s32[1024]{0:T(1024)S(1)} fusion(s32[5120]{0:T(1024)S(1)} %get-tuple-element.6, s32[1024]{0:T(1024)S(1)} %broadcast_clamp_fusion.1), kind=kCustom, calls=%fused_computation | custom fusion | bytes 12288 | tf_op jit(solution)/shard_map/jit(_take)/gather | solution.py:60
  49.9 140.1 %all-gather.2.cloned.1.call-done = bf16[4,5120,256]{2,0,1:T(4,128)(2,1)} async-done(((bf16[4,640,256]{2,0,1:T(4,128)(2,1)}), bf16[4,5120,256]{2,0,1:T(4,128)(2,1)}) %all-gather.2.cloned.1.call-update) | async-done | bytes 10485776 | tf_op jit(solution)/shard_map/all_gather | solution.py:72
  190.0 7.9 %gather_fusion.1 = bf16[1024,4,256]{2,1,0:T(4,128)(2,1)S(1)} fusion(bf16[4,5120,256]{2,0,1:T(4,128)(2,1)} %all-gather.2.cloned.1.call-done, s32[1024]{0:T(1024)S(1)} %broadcast_clamp_fusion), kind=kCustom, calls=%fused_computation.1 | custom fusion | bytes 4198400 | tf_op jit(solution)/shard_map/jit(_take)/gather | solution.py:74
  197.9 6.5 %select_bitcast_fusion = bf16[4,1024,256]{2,0,1:T(4,128)(2,1)S(1)} fusion(bf16[1024,4,256]{2,1,0:T(4,128)(2,1)S(1)} %gather_fusion.1, pred[1024]{0:T(1024)(128)(4,1)S(1)} %get-tuple-element.12, pred[1024]{0:T(1024)(128)(4,1)S(1)} %get-tuple-element.11), kind=kLoop, calls=%fused_computation.9 | loop fusion | flops 2097152 | bytes 4196352 | tf_op jit(solution)/shard_map/jit(_where)/select_n | solution.py:75
  204.4 0.5 slice_convert_fusion.1
  204.9 0.5 multiply_add_fusion
  205.5 2.2 maximum_reduce_fusion
  207.7 0.0 all-reduce.3.cloned.1.call-update
  207.7 31.7 %all-reduce.3.cloned.1.call-done = f32[512,256]{1,0:T(8,128)} async-done(((f32[512,256]{1,0:T(8,128)}), f32[512,256]{1,0:T(8,128)}) %all-reduce.3.cloned.1.call-update) | async-done | bytes 524304 | tf_op jit(solution)/shard_map/psum | solution.py:78
  239.4 1.9 broadcast_multiply_fusion
  (10 shorter events, 0.1 us)
Async XLA Ops:
  6.5 183.4 %all-gather.2.cloned.1.call-start = ((), (), s32[]{:S(2)}) async-start(), calls=%async_computation | async-start | bytes 11796480 | tf_op jit(solution)/shard_map/all_gather | solution.py:72
  13.5 1.7 slice-start
  34.4 2.2 copy-start
  34.5 9.0 %copy-start.1 = (s32[512,2]{0,1:T(2,128)S(1)}, s32[512,2]{0,1:T(2,128)}, u32[]{:S(2)}) copy-start(s32[512,2]{0,1:T(2,128)} %param.7) | copy-start | bytes 12292
  36.6 202.8 %all-reduce.3.cloned.1.call-start = ((), (), s32[]{:S(2)}) async-start(), calls=%async_computation.1 | async-start | bytes 1048576 | tf_op jit(solution)/shard_map/psum | solution.py:78
Sparse Core Ops, SparseCore 0:
  36.7 153.2 all-gather.1
  207.8 31.5 all-reduce.2
where the time goes:
time: 248 us
  waiting for transfers between devices  172 us (69%)
  local copies, waits for them, and re-layouts  29.1 us (12%)
  other arithmetic  21.8 us (9%)
  between operations  13.5 us (5%)
  matrix products  11.8 us (5%)
    all_gather x1, waiting for transfers between devices, local(): part_rows = lax.all_gather(whitened, 'chan', axis=1, tiled=True)  140 us
    psum x1, waiting for transfers between devices, local(): summed = lax.psum(stacked, 'tm')  31.7 us
    dot_general x1, matrix products, local(): spectrum = jnp.dot(filtered, dft_table, preferred_element_type=jnp.float32)  10.3 us
    gather x1, local copies, waits for them, and re-layouts, local(): jnp.take(part_rows, jnp.clip(wanted_ids, 0, part_rows.shape[1] - 1), axis=1)  7.92 us
    sort x1, other arithmetic, local(): rows_of = jnp.argsort(recorder_channel, stable=True)  6.76 us
    select_n x1, other arithmetic, local(): chosen = jnp.where(inside[None, :, None], taken, empty)  6.46 us
    gather x1, local copies, waits for them, and re-layouts, local(): wanted_ids = jnp.take(rows_of, endpoints)  6.37 us
    reshape x1, local copies, waits for them, and re-layouts, make_fir(): jnp.tile(padded, length)[:length * (period - 1)].reshape(length, period - 1)  6.35 us
  transfers between devices with their start and end apart: 2, of which 2 were waited for; matrix products, arithmetic and copies ran while one was open for 5% of the time, Pallas kernels for 0%

commit v1 on v0

--- a/solution.py
+++ b/solution.py
@@ -5,6 +5,24 @@
 
 NB = 128
 SMOOTH = 4
+
+
+def laid_out(blocks, dim):
+    shape = list(blocks.shape[1:])
+    shape[dim] *= blocks.shape[0]
+    return jnp.moveaxis(blocks, 0, dim).reshape(shape)
+
+
+def grow_blocks(value, axis):
+    devices = lax.axis_size(axis)
+    pieces = value[None]
+    for level in range(devices.bit_length() - 1):
+        bit = 1 << level
+        other = lax.ppermute(pieces, axis, [(i, i ^ bit) for i in range(devices)])
+        both = jnp.stack([pieces, other])
+        upper = lax.axis_index(axis) >> level & 1
+        pieces = jnp.where(upper == 0, both, both[::-1]).reshape(-1, *value.shape)
+    return pieces
 
 
 def make_fir(fir_taps, length):
@@ -69,7 +87,7 @@
     whitened = whiten(spectrum, smoother).reshape(windows, ch_dev, 2 * NB)
     pair_count = pairs.shape[0]
     empty = jnp.zeros((windows, 2 * pair_count, 2 * NB), jnp.bfloat16)
-    part_rows = lax.all_gather(whitened, "chan", axis=1, tiled=True)
+    part_rows = laid_out(grow_blocks(whitened, "chan"), 1)
     inside = (wanted_ids >= 0) & (wanted_ids < part_rows.shape[1])
     taken = jnp.take(part_rows, jnp.clip(wanted_ids, 0, part_rows.shape[1] - 1), axis=1)
     chosen = jnp.where(inside[None, :, None], taken, empty)

time: 248 us -> 464 us (1.87)
  waiting for transfers between devices: 172 us -> 331 us
  other arithmetic: 21.8 us -> 54.7 us
  local copies, waits for them, and re-layouts: 29.1 us -> 45.3 us
  starting transfers between devices: 0.04 us -> 7.3 us
    ppermute x0 -> x3, waiting for transfers between devices: none -> 297 us  [grow_blocks(): other = lax.ppermute(pieces, axis, [(i, i ^ bit) for i in range(devices)])]
    all_gather x1 -> x0, waiting for transfers between devices: 140 us -> none  [local(): part_rows = lax.all_gather(whitened, 'chan', axis=1, tiled=True)]
    select_n x0 -> x2, other arithmetic: none -> 16.1 us  [grow_blocks(): pieces = jnp.where(upper == 0, both, both[::-1]).reshape(-1, *value.shape)]
    another operation x1 -> x5, other arithmetic: 2.22 us -> 18.1 us  [the longest x4 15.9 us: grow_blocks(): both = jnp.stack([pieces, other])]
    reshape x1 -> x2, local copies, waits for them, and re-layouts: 2.09 us -> 17.5 us  [the longest x1 14.6 us: laid_out(): return jnp.moveaxis(blocks, 0, dim).reshape(shape)]
    ppermute x0 -> x3, starting transfers between devices: none -> 7.29 us  [grow_blocks(): other = lax.ppermute(pieces, axis, [(i, i ^ bit) for i in range(devices)])]
  transfers between devices with their start and end apart: 2 -> 4, of which waited for: 2 -> 4; matrix products, arithmetic and copies ran while one was open for 5% -> 3% of each run, Pallas kernels for 0% -> 0%
where the time goes in v1:
time: 464 us
  waiting for transfers between devices  331 us (71%)
  other arithmetic  54.7 us (12%)
  local copies, waits for them, and re-layouts  45.3 us (10%)
  between operations  13.5 us (3%)
  matrix products  11.8 us (3%)
  starting transfers between devices  7.3 us (2%)
    ppermute x3, waiting for transfers between devices, grow_blocks(): other = lax.ppermute(pieces, axis, [(i, i ^ bit) for i in range(devices)])  297 us
    psum x1, waiting for transfers between devices, local(): summed = lax.psum(stacked, 'tm')  34.3 us
    select_n x2, other arithmetic, grow_blocks(): pieces = jnp.where(upper == 0, both, both[::-1]).reshape(-1, *value.shape)  16.1 us
    another operation x4, other arithmetic, grow_blocks(): both = jnp.stack([pieces, other])  15.9 us
    reshape x1, local copies, waits for them, and re-layouts, laid_out(): return jnp.moveaxis(blocks, 0, dim).reshape(shape)  14.6 us
    dot_general x1, matrix products, local(): spectrum = jnp.dot(filtered, dft_table, preferred_element_type=jnp.float32)  10.3 us
  transfers between devices with their start and end apart: 4, of which 4 were waited for; matrix products, arithmetic and copies ran while one was open for 3% of the time, Pallas kernels for 0%

profile of v1, /device:TPU:0, one launch (start us, length us, event | category | flops | bytes accessed | tf_op | source)
XLA Modules:
  0.0 464.0 jit_solution(1699070462504247648)
XLA Ops:
  6.6 2.2 cosine_convert_fusion
  8.8 0.7 concatenate.69
  9.7 3.8 tile.11
  13.5 1.7 slice-done
  15.2 6.4 %reshape.241 = bf16[1024,1151]{1,0:T(8,128)(2,1)} reshape(bf16[1178624]{0:T(1024)(128)(2,1)S(1)} %slice-done) | data formatting | bytes 4714496 | tf_op jit(solution)/shard_map/reshape | solution.py:32
  21.5 10.3 %fusion.8 = f32[2560,256]{1,0:T(8,128)S(1)} fusion(bf16[2560,1024]{1,0:T(8,128)(2,1)} %bitcast.40, bf16[1024,1151]{1,0:T(8,128)(2,1)} %reshape.241, bf16[1024,128]{1,0:T(8,128)(2,1)S(1)} %get-tuple-element.18, bf16[1024,128]{1,0:T(8,128)(2,1)S(1)} %get-tuple-element.17), kind=kOutput, calls=%fused_computation.22 | convolution fusion | flops 6714556416 | bytes 10485760 | tf_op jit(solution)/shard_map/dot_general | solution.py:86
  31.9 0.5 fusion.19
  32.4 1.5 fusion
  33.9 1.5 fusion.1
  35.5 3.0 collective-permute-start
  38.5 29.0 %collective-permute-done = bf16[1,4,640,256]{3,2,1,0:T(8,128)(2,1)S(1)} collective-permute-done((bf16[1,4,640,256]{3,2,1,0:T(8,128)(2,1)}, bf16[1,4,640,256]{3,2,1,0:T(8,128)(2,1)S(1)}, u32[]{:S(2)}, u32[]{:S(2)}) %collective-permute-start) | collective-permute-done | bytes 1310752 | tf_op jit(solution)/shard_map/ppermute | solution.py:21
  67.5 1.6 pad_maximum_fusion.2
  69.0 2.3 fusion.4
  71.3 1.8 collective-permute-start.1
  73.1 56.6 %collective-permute-done.1 = bf16[2,4,640,256]{3,2,1,0:T(8,128)(2,1)} collective-permute-done((bf16[2,4,640,256]{3,2,1,0:T(8,128)(2,1)}, bf16[2,4,640,256]{3,2,1,0:T(8,128)(2,1)}, u32[]{:S(2)}, u32[]{:S(2)}) %collective-permute-start.1) | collective-permute-done | bytes 2621472 | tf_op jit(solution)/shard_map/ppermute | solution.py:21
  129.6 2.2 pad_maximum_fusion.1
  131.9 1.1 reverse_select_fusion.1
  133.0 2.9 copy.11
  135.9 0.9 copy-done
  136.8 2.5 collective-permute-start.2
  139.3 6.8 %sort.17 = (s32[5120]{0:T(1024)}, s32[5120]{0:T(1024)S(1)}) sort(s32[5120]{0:T(1024)S(1)} %copy-done.1, s32[5120]{0:T(1024)S(1)} %iota.22), dimensions={0}, to_apply=%region_0.0 | sort | flops 66560 | bytes 81920 | tf_op jit(solution)/shard_map/jit(argsort)/sort | solution.py:76
  146.1 6.2 %gather_fusion = s32[1024]{0:T(1024)S(1)} fusion(s32[5120]{0:T(1024)S(1)} %get-tuple-element.6, s32[1024]{0:T(1024)S(1)} %broadcast_clamp_fusion.1), kind=kCustom, calls=%fused_computation | custom fusion | bytes 12288 | tf_op jit(solution)/shard_map/jit(_take)/gather | solution.py:78
  152.3 211.4 %collective-permute-done.2 = bf16[4,4,640,256]{3,2,0,1:T(8,128)(2,1)} collective-permute-done((bf16[4,4,640,256]{3,2,0,1:T(8,128)(2,1)}, bf16[4,4,640,256]{3,2,0,1:T(8,128)(2,1)}, u32[]{:S(2)}, u32[]{:S(2)}) %collective-permute-start.2) | collective-permute-done | bytes 5242912 | tf_op jit(solution)/shard_map/ppermute | solution.py:21
  363.7 9.9 %pad_maximum_fusion = bf16[2,4,4,640,256]{4,3,1,0,2:T(8,128)(2,1)} fusion(bf16[1,4,4,640,256]{4,3,1,0,2:T(8,128)(2,1)} %bitcast.12, bf16[1,4,4,640,256]{4,3,2,1,0:T(8,128)(2,1)} %bitcast.32), kind=kLoop, calls=%fused_computation.3 | loop fusion | flops 20971520 | bytes 20971520 | tf_op jit(solution)/shard_map/stack | solution.py:22
  373.6 15.0 %reverse_select_fusion = bf16[2,4,4,640,256]{4,3,1,0,2:T(8,128)(2,1)} fusion(bf16[2,4,4,640,256]{4,3,1,0,2:T(8,128)(2,1)} %pad_maximum_fusion, pred[]{:T(512)S(6)} %eq.11), kind=kLoop, calls=%fused_computation.2 | loop fusion | flops 5242880 | bytes 20971520 | tf_op jit(solution)/shard_map/jit(_where)/select_n | solution.py:24
  388.6 14.6 %copy.13 = bf16[4,5120,256]{2,0,1:T(4,128)(2,1)} copy(bf16[4,5120,256]{2,1,0:T(8,128)(2,1)} %bitcast.33) | data formatting | bytes 20971520 | tf_op jit(solution)/shard_map/reshape | solution.py:13
  403.2 7.9 %gather_fusion.1 = bf16[1024,4,256]{2,1,0:T(4,128)(2,1)S(1)} fusion(bf16[4,5120,256]{2,0,1:T(4,128)(2,1)} %copy.13, s32[1024]{0:T(1024)S(1)} %broadcast_clamp_fusion), kind=kCustom, calls=%fused_computation.1 | custom fusion | bytes 4198400 | tf_op jit(solution)/shard_map/jit(_take)/gather | solution.py:92
  411.1 6.5 %select_bitcast_fusion = bf16[4,1024,256]{2,0,1:T(4,128)(2,1)S(1)} fusion(bf16[1024,4,256]{2,1,0:T(4,128)(2,1)S(1)} %gather_fusion.1, pred[1024]{0:T(1024)(128)(4,1)S(1)} %get-tuple-element.14, pred[1024]{0:T(1024)(128)(4,1)S(1)} %get-tuple-element.13), kind=kLoop, calls=%fused_computation.15 | loop fusion | flops 2097152 | bytes 4196352 | tf_op jit(solution)/shard_map/jit(_where)/select_n | solution.py:93
  418.2 0.5 multiply_add_fusion
  418.7 2.2 maximum_reduce_fusion
  420.9 34.3 %all-reduce.3.cloned.1.call-done = f32[512,256]{1,0:T(8,128)} async-done(((f32[512,256]{1,0:T(8,128)}), f32[512,256]{1,0:T(8,128)}) %all-reduce.3.cloned.1.call-update) | async-done | bytes 524304 | tf_op jit(solution)/shard_map/psum | solution.py:96
  455.3 1.9 broadcast_multiply_fusion
  (20 shorter events, 0.9 us)
Async XLA Ops:
  6.5 448.7 %all-reduce.3.cloned.1.call-start = ((), (), s32[]{:S(2)}) async-start(), calls=%async_computation | async-start | bytes 1048576 | tf_op jit(solution)/shard_map/psum | solution.py:96
  13.5 1.7 slice-start
  35.5 32.0 %collective-permute-start = (bf16[1,4,640,256]{3,2,1,0:T(8,128)(2,1)}, bf16[1,4,640,256]{3,2,1,0:T(8,128)(2,1)S(1)}, u32[]{:S(2)}, u32[]{:S(2)}) collective-permute-start(bf16[1,4,640,256]{3,2,1,0:T(8,128)(2,1)} %bitcast.5), channel_id=1, source_target_pairs={{0,1},{1,0},{2,3},{3,2},{4,5},{5,4},{6,7},{7,6},{8,9},{9,8},{10,11... | collective-permute-start | bytes 3932168 | tf_op jit(solution)/shard_map/ppermute | solution.py:21
  71.3 58.4 %collective-permute-start.1 = (bf16[2,4,640,256]{3,2,1,0:T(8,128)(2,1)}, bf16[2,4,640,256]{3,2,1,0:T(8,128)(2,1)}, u32[]{:S(2)}, u32[]{:S(2)}) collective-permute-start(bf16[2,4,640,256]{3,2,1,0:T(8,128)(2,1)} %get-tuple-element.10), channel_id=1, source_target_pairs={{0,2},{1,3},{2,0},{3,1},{4,6},{5,7},{6,4},{7,5},{8,10},{9,11},{10,... | collective-permute-start | bytes 7864328 | tf_op jit(solution)/shard_map/ppermute | solution.py:21
  132.9 3.9 copy-start
  132.9 6.4 %copy-start.1 = (s32[5120]{0:T(1024)S(1)}, s32[5120]{0:T(1024)}, u32[]{:S(2)}) copy-start(s32[5120]{0:T(1024)} %param.6) | copy-start | bytes 61444
  132.9 13.1 %copy-start.2 = (s32[512,2]{0,1:T(2,128)S(1)}, s32[512,2]{0,1:T(2,128)}, u32[]{:S(2)}) copy-start(s32[512,2]{0,1:T(2,128)} %param.7) | copy-start | bytes 12292
  136.8 226.9 %collective-permute-start.2 = (bf16[4,4,640,256]{3,2,0,1:T(8,128)(2,1)}, bf16[4,4,640,256]{3,2,0,1:T(8,128)(2,1)}, u32[]{:S(2)}, u32[]{:S(2)}) collective-permute-start(bf16[4,4,640,256]{3,2,0,1:T(8,128)(2,1)} %copy.11), channel_id=1, source_target_pairs={{0,4},{1,5},{2,6},{3,7},{4,0},{5,1},{6,2},{7,3},{8,12},{9,13},{10,... | collective-permute-start | bytes 15728648 | tf_op jit(solution)/shard_map/ppermute | solution.py:21
Sparse Core Ops, SparseCore 0:
  421.0 34.1 all-reduce.2
